TPU v7x, 32 devices: a whole 2x2x4 slice. The times are simulated.
32 devices in a mesh: tok: 4 (over y, x), col: 8 (over z, core).
Axes of the slice: x: 2, y: 2, z: 4, core: 2. Of those that a mesh axis runs over, the one named last changes fastest.
Arguments:
- activations: bfloat16 [8192, 8192], P('tok', 'col'), may hold values from -60 to 60, as said below
- weight: bfloat16 [8192, 8192], P('tok', 'col'), may hold values from -6 to 6
- keep_mask: int32 [8192, 8192], P('tok', 'col'), may hold values from 0 to 1
Outputs:
- new_weight: bfloat16 [8192, 8192], P('tok', 'col')
Inputs may be any that keep to these rules, and one draw needn't show every extreme that they name: activations of calibration tokens.
All inputs are finite; a program needn't handle non-finite values.
Results may differ from a plain program's by a relative error of at most 0.00115.
Values may be sent and summed in bfloat16 or wider, within the bound.
No kernel may reach another device: no remote copies, remote signals or barrier semaphores. Data moves between devices by JAX's collectives and lax.ppermute only.
A program may use at most 128 MiB of HBM per device.

v0:
```python
import jax
import jax.numpy as jnp
from jax import lax
from jax.sharding import PartitionSpec as P

B = 1024
ITERS = 4


def per_device(activations, weight, keep_mask):
    highest = lax.Precision.HIGHEST
    n_col = lax.axis_size("col")
    n_tok = lax.axis_size("tok")
    tok_rows = activations.shape[0]
    panel_width = B // n_col
    total_count = tok_rows * n_tok
    partial_panel = lax.dot_general(
        activations,
        lax.all_gather(activations[:, :panel_width], "col", axis=1, tiled=True),
        (((0,), (0,)), ((), ())),
        preferred_element_type=jnp.float32,
    )
    block_part = lax.psum(partial_panel[:panel_width], "tok") / total_count
    diagonal_block = lax.all_gather(block_part, "col", axis=0, tiled=True)
    identity = jnp.eye(B, dtype=jnp.float32)
    damping = 0.01 * jnp.mean(jnp.diagonal(diagonal_block))
    damped = diagonal_block + damping * identity
    frobenius = jnp.sqrt(jnp.sum(damped * damped))
    col_index = lax.axis_index("col")
    row_ids = col_index * panel_width + lax.iota(jnp.int32, panel_width)
    iterate = (row_ids[:, None] == lax.iota(jnp.int32, B)[None, :]).astype(jnp.float32) / frobenius
    for sweep in range(ITERS):
        if sweep == 0:
            whole = identity / frobenius
        else:
            whole = lax.all_gather(iterate.astype(jnp.bfloat16), "col", axis=0, tiled=True).astype(
                iterate.dtype
            )
        product = jnp.dot(iterate, damped, precision=highest)
        iterate = 2.0 * iterate - jnp.dot(product, whole, precision=highest)
    inverse = lax.all_gather(iterate, "col", axis=0, tiled=True)
    remainder = lax.psum(partial_panel[panel_width:], "tok") / total_count
    hessian_panel = jnp.concatenate([block_part, remainder], axis=0)
    pruned = jnp.where(
        keep_mask[:, :panel_width] == 0, weight[:, :panel_width], jnp.zeros((), jnp.bfloat16)
    )
    pruned_panel = lax.all_gather(pruned, "col", axis=1, tiled=True).astype(jnp.float32)
    factor_rows = jnp.dot(pruned_panel, inverse, precision=highest)
    correction = lax.dot_general(
        factor_rows, hessian_panel, (((1,), (1,)), ((), ())), precision=highest
    )
    kept = keep_mask.astype(jnp.float32)
    return (kept * (weight.astype(jnp.float32) - correction)).astype(jnp.bfloat16)


def solution(mesh):
    return jax.shard_map(
        per_device,
        mesh=mesh,
        in_specs=(P("tok", "col"), P("tok", "col"), P("tok", "col")),
        out_specs=P("tok", "col"),
        check_vma=False,
    )
```

profile of v0, /device:TPU:0, one launch (start us, length us, event | category | flops | bytes accessed | tf_op | source)
XLA Modules:
  0.0 493.3 jit_solution(1033233946870937970)
XLA Ops:
  6.5 1.9 slice.17
  8.5 51.0 %all-gather.10.cloned.1.call-done = bf16[2048,1024]{1,0:T(8,128)(2,1)} async-done(((bf16[2048,128]{1,0:T(8,128)(2,1)}), bf16[2048,1024]{1,0:T(8,128)(2,1)}) %all-gather.10.cloned.1.call-update) | async-done | bytes 4194320 | tf_op jit(solution)/shard_map/all_gather | solution.py:19
  59.5 7.6 %fusion.31 = f32[1024,1024]{1,0:T(8,128)S(1)} fusion(bf16[2048,1024]{1,0:T(8,128)(2,1)} %param.3, bf16[2048,1024]{1,0:T(8,128)(2,1)} %all-gather.10.cloned.1.call-done), kind=kOutput, calls=%fused_computation.42 | convolution fusion | flops 4294967296 | bytes 12582912 | tf_op jit(solution)/shard_map/dot_general | solution.py:17
  67.1 0.8 slice.22
  67.9 2.3 slice.23
  70.3 101.9 %all-reduce.3.cloned.1.call-done = (f32[128,1024]{1,0:T(8,128)}, f32[896,1024]{1,0:T(8,128)}) async-done(((f32[128,1024]{1,0:T(8,128)}, f32[896,1024]{1,0:T(8,128)}), (f32[128,1024]{1,0:T(8,128)}, f32[896,1024]{1,0:T(8,128)})) %all-reduce.3.cloned.1.call-update) | async-done | bytes 4194320 | tf_op jit(solution)/shard_map/psum | solution.py:23
  172.2 1.9 broadcast_multiply_fusion.1
  174.2 46.9 %all-gather.12.cloned.1.call-done = f32[1024,1024]{1,0:T(8,128)} async-done(((f32[128,1024]{1,0:T(8,128)}), f32[1024,1024]{1,0:T(8,128)}) %all-gather.12.cloned.1.call-update) | async-done | bytes 4194320 | tf_op jit(solution)/shard_map/all_gather | solution.py:24
  221.2 17.1 %gather_fusion = f32[1024]{0:T(1024)S(1)} fusion(f32[1024,1024]{1,0:T(8,128)} %all-gather.12.cloned.1.call-done, s32[1024]{0:T(1024)S(1)} %bitcast.16), kind=kCustom, calls=%fused_computation | custom fusion | bytes 16384 | tf_op jit(solution)/shard_map/jit(diagonal)/cond/branch_0_fun/gather | solution.py:26
  238.2 0.6 reduce_sum.18
  239.5 3.9 multiply_reduce_fusion
  244.0 4.7 fusion.16
  248.8 2.5 fusion.28
  251.3 0.0 all-gather.16.cloned.1.call-start
  251.3 4.7 fusion.15
  256.0 23.4 %all-gather.14.cloned.1.call-done = bf16[1024,1024]{1,0:T(8,128)(2,1)} async-done(((bf16[128,1024]{1,0:T(8,128)(2,1)}), bf16[1024,1024]{1,0:T(8,128)(2,1)}) %all-gather.14.cloned.1.call-update) | async-done | bytes 2097168 | tf_op jit(solution)/shard_map/all_gather | solution.py:36
  279.4 3.3 fusion.29
  282.8 0.2 all-gather.18.cloned.1.call-start
  283.0 4.7 fusion.14
  287.7 23.8 %all-gather.16.cloned.1.call-done = bf16[1024,1024]{1,0:T(8,128)(2,1)} async-done(((bf16[128,1024]{1,0:T(8,128)(2,1)}), bf16[1024,1024]{1,0:T(8,128)(2,1)}) %all-gather.16.cloned.1.call-update) | async-done | bytes 2097168 | tf_op jit(solution)/shard_map/all_gather | solution.py:36
  311.5 3.3 fusion.30
  314.9 0.0 all-gather.8.cloned.1.call-start
  314.9 2.3 fusion.17
  317.2 0.0 all-gather.20.cloned.1.call-start
  317.3 4.7 fusion.13
  322.0 21.6 %all-gather.18.cloned.1.call-done = bf16[1024,1024]{1,0:T(8,128)(2,1)} async-done(((bf16[128,1024]{1,0:T(8,128)(2,1)}), bf16[1024,1024]{1,0:T(8,128)(2,1)}) %all-gather.18.cloned.1.call-update) | async-done | bytes 2097168 | tf_op jit(solution)/shard_map/all_gather | solution.py:36
  343.6 3.4 convolution_subtract_fusion
  347.0 4.6 broadcast_multiply_fusion
  351.6 40.8 %all-gather.8.cloned.1.call-done = bf16[2048,1024]{1,0:T(8,128)(2,1)} async-done(((bf16[2048,128]{1,0:T(8,128)(2,1)}), bf16[2048,1024]{1,0:T(8,128)(2,1)}) %all-gather.8.cloned.1.call-update) | async-done | bytes 4194320 | tf_op jit(solution)/shard_map/all_gather | solution.py:47
  392.4 46.7 %all-gather.20.cloned.1.call-done = f32[1024,1024]{1,0:T(8,128)} async-done(((f32[128,1024]{1,0:T(8,128)}), f32[1024,1024]{1,0:T(8,128)}) %all-gather.20.cloned.1.call-update) | async-done | bytes 4194320 | tf_op jit(solution)/shard_map/all_gather | solution.py:41
  439.1 16.8 %fusion.32 = f32[2048,1024]{1,0:T(8,128)S(1)} fusion(bf16[2048,1024]{1,0:T(8,128)(2,1)} %all-gather.8.cloned.1.call-done, f32[1024,1024]{1,0:T(8,128)} %all-gather.20.cloned.1.call-done), kind=kOutput, calls=%fused_computation.43 | convolution fusion | flops 25769803776 | bytes 16777216 | tf_op jit(solution)/shard_map/dot_general | solution.py:48
  455.9 30.5 %multiply_convert_fusion = bf16[2048,1024]{1,0:T(8,128)(2,1)} fusion(bf16[2048,1024]{1,0:T(8,128)(2,1)S(1)} %copy-done.2, s32[2048,1024]{1,0:T(8,128)} %param.5, f32[2048,1024]{1,0:T(8,128)S(1)} %fusion.32, f32[896,1024]{1,0:T(8,128)S(1)} %copy-done, f32[128,1024]{1,0:T(8,128)S(1)} %copy-done.1), kind=kOutput, calls=%fused_computation.1 | convolution fusion | flops 25781338112 | bytes 29360128 | tf_op jit(solution)/shard_map/dot_general | solution.py:49
  (20 shorter events, 0.3 us)
Async XLA Ops:
  6.5 53.0 %all-gather.10.cloned.1.call-start = ((), (), s32[]{:S(2)}) async-start(), calls=%async_computation.1 | async-start | bytes 4718592 | tf_op jit(solution)/shard_map/all_gather | solution.py:19
  8.4 163.8 %all-reduce.3.cloned.1.call-start = ((), (), s32[]{:S(2)}) async-start(), calls=%async_computation.7 | async-start | bytes 8388608 | tf_op jit(solution)/shard_map/psum | solution.py:23
  70.2 150.9 %all-gather.12.cloned.1.call-start = ((), (), s32[]{:S(2)}) async-start(), calls=%async_computation.2 | async-start | bytes 4718592 | tf_op jit(solution)/shard_map/all_gather | solution.py:24
  174.1 105.3 %all-gather.14.cloned.1.call-start = ((), (), s32[]{:S(2)}) async-start(), calls=%async_computation.3 | async-start | bytes 2359296 | tf_op jit(solution)/shard_map/all_gather | solution.py:36
  251.3 60.2 %all-gather.16.cloned.1.call-start = ((), (), s32[]{:S(2)}) async-start(), calls=%async_computation.4 | async-start | bytes 2359296 | tf_op jit(solution)/shard_map/all_gather | solution.py:36
  282.8 60.8 %all-gather.18.cloned.1.call-start = ((), (), s32[]{:S(2)}) async-start(), calls=%async_computation.5 | async-start | bytes 2359296 | tf_op jit(solution)/shard_map/all_gather | solution.py:36
  314.9 77.5 %all-gather.8.cloned.1.call-start = ((), (), s32[]{:S(2)}) async-start(), calls=%async_computation | async-start | bytes 4718592 | tf_op jit(solution)/shard_map/all_gather | solution.py:47
  317.2 121.8 %all-gather.20.cloned.1.call-start = ((), (), s32[]{:S(2)}) async-start(), calls=%async_computation.6 | async-start | bytes 4718592 | tf_op jit(solution)/shard_map/all_gather | solution.py:41
  351.6 104.3 %copy-start.1 = (f32[128,1024]{1,0:T(8,128)S(1)}, f32[128,1024]{1,0:T(8,128)}, u32[]{:S(2)}) copy-start(f32[128,1024]{1,0:T(8,128)} %broadcast_multiply_fusion.1) | copy-start | bytes 1572868
  439.1 16.8 %copy-start = (f32[896,1024]{1,0:T(8,128)S(1)}, f32[896,1024]{1,0:T(8,128)}, u32[]{:S(2)}) copy-start(f32[896,1024]{1,0:T(8,128)} %broadcast_multiply_fusion) | copy-start | bytes 11010052
  439.1 16.8 %copy-start.2 = (bf16[2048,1024]{1,0:T(8,128)(2,1)S(1)}, bf16[2048,1024]{1,0:T(8,128)(2,1)}, u32[]{:S(2)}) copy-start(bf16[2048,1024]{1,0:T(8,128)(2,1)} %param.4) | copy-start | bytes 12582916
Sparse Core Ops, SparseCore 0:
  8.9 50.5 all-gather.9
  70.3 101.8 all-reduce.2
  174.3 46.8 all-gather.11
  251.4 27.9 all-gather.13
  282.9 28.6 all-gather.15
  315.0 28.5 all-gather.17
  345.2 47.2 all-gather.7
  394.0 45.0 all-gather.19
where the time goes:
time: 494 us; the launch traced here: 493 us
  waiting for transfers between devices  356 us (72%)
  matrix products  86.3 us (17%)
  local copies, waits for them, and re-layouts  22.1 us (4%)
  between operations  14.9 us (3%)
  other arithmetic  13.3 us (3%)
    psum x1, waiting for transfers between devices, per_device(): block_part = lax.psum(partial_panel[:panel_width], 'tok') / total_count  102 us
    all_gather x3, waiting for transfers between devices, per_device(): lax.all_gather(iterate.astype(jnp.bfloat16), 'col', axis=0, tiled=True)  68.8 us
    all_gather x1, waiting for transfers between devices, per_device(): lax.all_gather(activations[:, :panel_width], 'col', axis=1, tiled=True)  51 us
    all_gather x1, waiting for transfers between devices, per_device(): diagonal_block = lax.all_gather(block_part, 'col', axis=0, tiled=True)  46.9 us
    all_gather x1, waiting for transfers between devices, per_device(): inverse = lax.all_gather(iterate, 'col', axis=0, tiled=True)  46.7 us
    all_gather x1, waiting for transfers between devices, per_device(): lax.all_gather(pruned, 'col', axis=1, tiled=True).astype(jnp.float32)  40.8 us
    dot_general x1, matrix products, per_device(): lax.dot_general(factor_rows, hessian_panel, (((1,), (1,)), ((), ())), pre...  30.5 us
    dot_general x4, matrix products, per_device(): product = jnp.dot(iterate, damped, precision=highest)  18.8 us
  transfers between devices with their start and end apart: 8, of which 8 were waited for; matrix products, arithmetic and copies ran while one was open for 5% of the time, Pallas kernels for 0%

commit v1 on v0

--- a/solution.py
+++ b/solution.py
@@ -21,7 +21,16 @@
         preferred_element_type=jnp.float32,
     )
     block_part = lax.psum(partial_panel[:panel_width], "tok") / total_count
-    diagonal_block = lax.all_gather(block_part, "col", axis=0, tiled=True)
+    n_chips = lax.axis_size("col")
+    part_now = sorted(((num, (num + 1) % n_chips) for num in range(n_chips)))
+    out_arr = block_part
+    line_up = [out_arr]
+    for nth in tuple(range(1, n_chips)):
+        out_arr = lax.ppermute(out_arr, "col", part_now)
+        line_up.insert(0, out_arr)
+    r2 = jnp.concatenate(line_up, 0)
+    step_out = lax.axis_index("col") + 1
+    diagonal_block = jnp.roll(r2, step_out * block_part.shape[0], 0)
     identity = jnp.eye(B, dtype=jnp.float32)
     damping = 0.01 * jnp.mean(jnp.diagonal(diagonal_block))
     damped = diagonal_block + damping * identity

time: 494 us -> 528 us (1.069)
  waiting for transfers between devices: 356 us -> 380 us
  local copies, waits for them, and re-layouts: 22.1 us -> 31.5 us
    ppermute x0 -> x7, waiting for transfers between devices: none -> 73.2 us  [per_device(): out_arr = lax.ppermute(out_arr, 'col', part_now)]
    all_gather x1 -> x0, waiting for transfers between devices: 46.9 us -> none  [per_device(): diagonal_block = lax.all_gather(block_part, 'col', axis=0, tiled=True)]
    unnamed x6 -> x26, local copies, waits for them, and re-layouts: 0.01 us -> 6.7 us
  transfers between devices with their start and end apart: 8 -> 14, of which waited for: 8 -> 14; matrix products, arithmetic and copies ran while one was open for 5% -> 5% of each run, Pallas kernels for 0% -> 0%
where the time goes in v1:
time: 528 us; the launch traced here: 527 us
  waiting for transfers between devices  380 us (72%)
  matrix products  86.3 us (16%)
  local copies, waits for them, and re-layouts  31.5 us (6%)
  between operations  15 us (3%)
  other arithmetic  12.8 us (2%)
    psum x1, waiting for transfers between devices, per_device(): block_part = lax.psum(partial_panel[:panel_width], 'tok') / total_count  102 us
    ppermute x7, waiting for transfers between devices, per_device(): out_arr = lax.ppermute(out_arr, 'col', part_now)  73.2 us
    all_gather x3, waiting for transfers between devices, per_device(): lax.all_gather(iterate.astype(jnp.bfloat16), 'col', axis=0, tiled=True)  66.8 us
    all_gather x1, waiting for transfers between devices, per_device(): lax.all_gather(activations[:, :panel_width], 'col', axis=1, tiled=True)  51 us
    all_gather x1, waiting for transfers between devices, per_device(): inverse = lax.all_gather(iterate, 'col', axis=0, tiled=True)  46.7 us
    all_gather x1, waiting for transfers between devices, per_device(): lax.all_gather(pruned, 'col', axis=1, tiled=True).astype(jnp.float32)  40.7 us
    dot_general x1, matrix products, per_device(): lax.dot_general(factor_rows, hessian_panel, (((1,), (1,)), ((), ())), pre...  30.6 us
    dot_general x4, matrix products, per_device(): product = jnp.dot(iterate, damped, precision=highest)  18.8 us
  transfers between devices with their start and end apart: 14, of which 14 were waited for; matrix products, arithmetic and copies ran while one was open for 5% of the time, Pallas kernels for 0%

profile of v1, /device:TPU:0, one launch (start us, length us, event | category | flops | bytes accessed | tf_op | source)
XLA Modules:
  0.0 526.8 jit_solution(8335016707694100384)
XLA Ops:
  8.5 51.0 %all-gather.9.cloned.1.call-done = bf16[2048,1024]{1,0:T(8,128)(2,1)} async-done(((bf16[2048,128]{1,0:T(8,128)(2,1)}), bf16[2048,1024]{1,0:T(8,128)(2,1)}) %all-gather.9.cloned.1.call-update) | async-done | bytes 4194320 | tf_op jit(solution)/shard_map/all_gather | solution.py:19
  59.5 7.6 %fusion.31 = f32[1024,1024]{1,0:T(8,128)S(1)} fusion(bf16[2048,1024]{1,0:T(8,128)(2,1)} %param.3, bf16[2048,1024]{1,0:T(8,128)(2,1)} %all-gather.9.cloned.1.call-done), kind=kOutput, calls=%fused_computation.59 | convolution fusion | flops 4294967296 | bytes 12582912 | tf_op jit(solution)/shard_map/dot_general | solution.py:17
  67.1 2.3 slice.23
  70.3 101.9 %all-reduce.3.cloned.1.call-done = (f32[128,1024]{1,0:T(8,128)}, f32[896,1024]{1,0:T(8,128)}) async-done(((f32[128,1024]{1,0:T(8,128)}, f32[896,1024]{1,0:T(8,128)}), (f32[128,1024]{1,0:T(8,128)}, f32[896,1024]{1,0:T(8,128)})) %all-reduce.3.cloned.1.call-update) | async-done | bytes 4194320 | tf_op jit(solution)/shard_map/psum | solution.py:23
  173.4 10.4 %collective-permute-done = f32[128,1024]{1,0:T(8,128)S(1)} collective-permute-done((f32[128,1024]{1,0:T(8,128)S(1)}, f32[128,1024]{1,0:T(8,128)S(1)}, u32[]{:S(2)}, u32[]{:S(2)}) %collective-permute-start) | collective-permute-done | bytes 524320 | tf_op jit(solution)/shard_map/ppermute | solution.py:29
  183.8 10.4 %collective-permute-done.1 = f32[128,1024]{1,0:T(8,128)S(1)} collective-permute-done((f32[128,1024]{1,0:T(8,128)S(1)}, f32[128,1024]{1,0:T(8,128)S(1)}, u32[]{:S(2)}, u32[]{:S(2)}) %collective-permute-start.1) | collective-permute-done | bytes 524320 | tf_op jit(solution)/shard_map/ppermute | solution.py:29
  194.2 10.4 %collective-permute-done.2 = f32[128,1024]{1,0:T(8,128)S(1)} collective-permute-done((f32[128,1024]{1,0:T(8,128)S(1)}, f32[128,1024]{1,0:T(8,128)S(1)}, u32[]{:S(2)}, u32[]{:S(2)}) %collective-permute-start.2) | collective-permute-done | bytes 524320 | tf_op jit(solution)/shard_map/ppermute | solution.py:29
  204.6 10.4 %collective-permute-done.3 = f32[128,1024]{1,0:T(8,128)S(1)} collective-permute-done((f32[128,1024]{1,0:T(8,128)S(1)}, f32[128,1024]{1,0:T(8,128)S(1)}, u32[]{:S(2)}, u32[]{:S(2)}) %collective-permute-start.3) | collective-permute-done | bytes 524320 | tf_op jit(solution)/shard_map/ppermute | solution.py:29
  215.0 10.4 %collective-permute-done.4 = f32[128,1024]{1,0:T(8,128)S(1)} collective-permute-done((f32[128,1024]{1,0:T(8,128)S(1)}, f32[128,1024]{1,0:T(8,128)S(1)}, u32[]{:S(2)}, u32[]{:S(2)}) %collective-permute-start.4) | collective-permute-done | bytes 524320 | tf_op jit(solution)/shard_map/ppermute | solution.py:29
  225.4 10.5 %collective-permute-done.5 = f32[128,1024]{1,0:T(8,128)} collective-permute-done((f32[128,1024]{1,0:T(8,128)S(1)}, f32[128,1024]{1,0:T(8,128)}, u32[]{:S(2)}, u32[]{:S(2)}) %collective-permute-start.5) | collective-permute-done | bytes 524320 | tf_op jit(solution)/shard_map/ppermute | solution.py:29
  236.0 10.7 %collective-permute-done.6 = f32[128,1024]{1,0:T(8,128)} collective-permute-done((f32[128,1024]{1,0:T(8,128)}, f32[128,1024]{1,0:T(8,128)}, u32[]{:S(2)}, u32[]{:S(2)}) %collective-permute-start.6) | collective-permute-done | bytes 524320 | tf_op jit(solution)/shard_map/ppermute | solution.py:29
  251.6 2.5 constant_dynamic-slice_fusion
  254.1 2.0 copy-done
  256.1 17.2 %gather_fusion = f32[1024]{0:T(1024)S(1)} fusion(f32[1024,1024]{1,0:T(8,128)} %constant_dynamic-slice_fusion, s32[1024]{0:T(1024)S(1)} %bitcast.16), kind=kCustom, calls=%fused_computation | custom fusion | bytes 16384 | tf_op jit(solution)/shard_map/jit(diagonal)/cond/branch_0_fun/gather | solution.py:35
  274.6 3.9 multiply_reduce_fusion
  279.2 4.7 fusion.16
  283.9 2.5 fusion.28
  286.7 4.7 fusion.15
  291.4 21.6 %all-gather.11.cloned.1.call-done = bf16[1024,1024]{1,0:T(8,128)(2,1)} async-done(((bf16[128,1024]{1,0:T(8,128)(2,1)}), bf16[1024,1024]{1,0:T(8,128)(2,1)}) %all-gather.11.cloned.1.call-update) | async-done | bytes 2097168 | tf_op jit(solution)/shard_map/all_gather | solution.py:45
  313.0 3.3 fusion.29
  316.4 4.7 fusion.14
  321.1 24.0 %all-gather.13.cloned.1.call-done = bf16[1024,1024]{1,0:T(8,128)(2,1)} async-done(((bf16[128,1024]{1,0:T(8,128)(2,1)}), bf16[1024,1024]{1,0:T(8,128)(2,1)}) %all-gather.13.cloned.1.call-update) | async-done | bytes 2097168 | tf_op jit(solution)/shard_map/all_gather | solution.py:45
  345.1 3.3 fusion.30
  348.5 2.4 fusion.17
  351.1 4.7 fusion.13
  355.8 21.3 %all-gather.15.cloned.1.call-done = bf16[1024,1024]{1,0:T(8,128)(2,1)} async-done(((bf16[128,1024]{1,0:T(8,128)(2,1)}), bf16[1024,1024]{1,0:T(8,128)(2,1)}) %all-gather.15.cloned.1.call-update) | async-done | bytes 2097168 | tf_op jit(solution)/shard_map/all_gather | solution.py:45
  377.1 3.4 convolution_subtract_fusion
  380.6 4.6 broadcast_multiply_fusion
  385.1 40.7 %all-gather.7.cloned.1.call-done = bf16[2048,1024]{1,0:T(8,128)(2,1)} async-done(((bf16[2048,128]{1,0:T(8,128)(2,1)}), bf16[2048,1024]{1,0:T(8,128)(2,1)}) %all-gather.7.cloned.1.call-update) | async-done | bytes 4194320 | tf_op jit(solution)/shard_map/all_gather | solution.py:56
  425.8 46.7 %all-gather.17.cloned.1.call-done = f32[1024,1024]{1,0:T(8,128)} async-done(((f32[128,1024]{1,0:T(8,128)}), f32[1024,1024]{1,0:T(8,128)}) %all-gather.17.cloned.1.call-update) | async-done | bytes 4194320 | tf_op jit(solution)/shard_map/all_gather | solution.py:50
  472.5 16.8 %fusion.32 = f32[2048,1024]{1,0:T(8,128)S(1)} fusion(bf16[2048,1024]{1,0:T(8,128)(2,1)} %all-gather.7.cloned.1.call-done, f32[1024,1024]{1,0:T(8,128)} %all-gather.17.cloned.1.call-done), kind=kOutput, calls=%fused_computation.60 | convolution fusion | flops 25769803776 | bytes 16777216 | tf_op jit(solution)/shard_map/dot_general | solution.py:57
  489.3 30.6 %multiply_convert_fusion = bf16[2048,1024]{1,0:T(8,128)(2,1)} fusion(bf16[2048,1024]{1,0:T(8,128)(2,1)S(1)} %copy-done.5, s32[2048,1024]{1,0:T(8,128)} %param.5, f32[2048,1024]{1,0:T(8,128)S(1)} %fusion.32, f32[896,1024]{1,0:T(8,128)S(1)} %copy-done.2, f32[128,1024]{1,0:T(8,128)S(1)} %copy-done.4), kind=kOutput, calls=%fused_computation.1 | convolution fusion | flops 25781338112 | bytes 29360128 | tf_op jit(solution)/shard_map/dot_general | solution.py:58
  (54 shorter events, 10.2 us)
Async XLA Ops:
  6.5 53.0 %all-gather.9.cloned.1.call-start = ((), (), s32[]{:S(2)}) async-start(), calls=%async_computation.1 | async-start | bytes 4718592 | tf_op jit(solution)/shard_map/all_gather | solution.py:19
  8.4 163.8 %all-reduce.3.cloned.1.call-start = ((), (), s32[]{:S(2)}) async-start(), calls=%async_computation.6 | async-start | bytes 8388608 | tf_op jit(solution)/shard_map/psum | solution.py:23
  70.2 242.8 %all-gather.11.cloned.1.call-start = ((), (), s32[]{:S(2)}) async-start(), calls=%async_computation.2 | async-start | bytes 2359296 | tf_op jit(solution)/shard_map/all_gather | solution.py:45
  172.2 76.9 %copy-start.1 = (f32[128,1024]{1,0:T(8,128)S(1)}, f32[128,1024]{1,0:T(8,128)}, u32[]{:S(2)}) copy-start(f32[128,1024]{1,0:T(8,128)} %get-tuple-element.5) | copy-start | bytes 1572868
  173.4 62.6 %copy-start.3 = (f32[128,1024]{1,0:T(8,128)}, f32[128,1024]{1,0:T(8,128)S(1)}, u32[]{:S(2)}) copy-start(f32[128,1024]{1,0:T(8,128)S(1)} %broadcast_multiply_fusion.1) | copy-start | bytes 1572868
  173.4 10.5 %collective-permute-start = (f32[128,1024]{1,0:T(8,128)S(1)}, f32[128,1024]{1,0:T(8,128)S(1)}, u32[]{:S(2)}, u32[]{:S(2)}) collective-permute-start(f32[128,1024]{1,0:T(8,128)S(1)} %broadcast_multiply_fusion.1), channel_id=1, source_target_pairs={{0,1},{1,2},{2,3},{3,4},{4,5},{5,6},{6,7},{7,0},{8,9},{9,10},{10,1... | collective-permute-start | bytes 1572872 | tf_op jit(solution)/shard_map/ppermute | solution.py:29
  183.8 10.4 %collective-permute-start.1 = (f32[128,1024]{1,0:T(8,128)S(1)}, f32[128,1024]{1,0:T(8,128)S(1)}, u32[]{:S(2)}, u32[]{:S(2)}) collective-permute-start(f32[128,1024]{1,0:T(8,128)S(1)} %collective-permute-done), channel_id=1, source_target_pairs={{0,1},{1,2},{2,3},{3,4},{4,5},{5,6},{6,7},{7,0},{8,9},{9,10},{10,1... | collective-permute-start | bytes 1572872 | tf_op jit(solution)/shard_map/ppermute | solution.py:29
  194.2 10.4 %collective-permute-start.2 = (f32[128,1024]{1,0:T(8,128)S(1)}, f32[128,1024]{1,0:T(8,128)S(1)}, u32[]{:S(2)}, u32[]{:S(2)}) collective-permute-start(f32[128,1024]{1,0:T(8,128)S(1)} %collective-permute-done.1), channel_id=1, source_target_pairs={{0,1},{1,2},{2,3},{3,4},{4,5},{5,6},{6,7},{7,0},{8,9},{9,10},{10,1... | collective-permute-start | bytes 1572872 | tf_op jit(solution)/shard_map/ppermute | solution.py:29
  204.6 10.4 %collective-permute-start.3 = (f32[128,1024]{1,0:T(8,128)S(1)}, f32[128,1024]{1,0:T(8,128)S(1)}, u32[]{:S(2)}, u32[]{:S(2)}) collective-permute-start(f32[128,1024]{1,0:T(8,128)S(1)} %collective-permute-done.2), channel_id=1, source_target_pairs={{0,1},{1,2},{2,3},{3,4},{4,5},{5,6},{6,7},{7,0},{8,9},{9,10},{10,1... | collective-permute-start | bytes 1572872 | tf_op jit(solution)/shard_map/ppermute | solution.py:29
  215.0 10.4 %collective-permute-start.4 = (f32[128,1024]{1,0:T(8,128)S(1)}, f32[128,1024]{1,0:T(8,128)S(1)}, u32[]{:S(2)}, u32[]{:S(2)}) collective-permute-start(f32[128,1024]{1,0:T(8,128)S(1)} %collective-permute-done.3), channel_id=1, source_target_pairs={{0,1},{1,2},{2,3},{3,4},{4,5},{5,6},{6,7},{7,0},{8,9},{9,10},{10,1... | collective-permute-start | bytes 1572872 | tf_op jit(solution)/shard_map/ppermute | solution.py:29
  225.4 10.5 %collective-permute-start.5 = (f32[128,1024]{1,0:T(8,128)S(1)}, f32[128,1024]{1,0:T(8,128)}, u32[]{:S(2)}, u32[]{:S(2)}) collective-permute-start(f32[128,1024]{1,0:T(8,128)S(1)} %collective-permute-done.4), channel_id=1, source_target_pairs={{0,1},{1,2},{2,3},{3,4},{4,5},{5,6},{6,7},{7,0},{8,9},{9,10},{10,1... | collective-permute-start | bytes 1572872 | tf_op jit(solution)/shard_map/ppermute | solution.py:29
  236.0 10.7 %collective-permute-start.6 = (f32[128,1024]{1,0:T(8,128)}, f32[128,1024]{1,0:T(8,128)}, u32[]{:S(2)}, u32[]{:S(2)}) collective-permute-start(f32[128,1024]{1,0:T(8,128)} %collective-permute-done.5), channel_id=1, source_target_pairs={{0,1},{1,2},{2,3},{3,4},{4,5},{5,6},{6,7},{7,0},{8,9},{9,10},{10,1... | collective-permute-start | bytes 1572872 | tf_op jit(solution)/shard_map/ppermute | solution.py:29
  251.6 4.5 copy-start
  286.5 58.6 %all-gather.13.cloned.1.call-start = ((), (), s32[]{:S(2)}) async-start(), calls=%async_computation.3 | async-start | bytes 2359296 | tf_op jit(solution)/shard_map/all_gather | solution.py:45
  316.4 60.8 %all-gather.15.cloned.1.call-start = ((), (), s32[]{:S(2)}) async-start(), calls=%async_computation.4 | async-start | bytes 2359296 | tf_op jit(solution)/shard_map/all_gather | solution.py:45
  348.4 77.4 %all-gather.7.cloned.1.call-start = ((), (), s32[]{:S(2)}) async-start(), calls=%async_computation | async-start | bytes 4718592 | tf_op jit(solution)/shard_map/all_gather | solution.py:56
  350.9 121.6 %all-gather.17.cloned.1.call-start = ((), (), s32[]{:S(2)}) async-start(), calls=%async_computation.5 | async-start | bytes 4718592 | tf_op jit(solution)/shard_map/all_gather | solution.py:50
  385.1 104.2 %copy-start.4 = (f32[128,1024]{1,0:T(8,128)S(1)}, f32[128,1024]{1,0:T(8,128)}, u32[]{:S(2)}) copy-start(f32[128,1024]{1,0:T(8,128)} %copy-done.3) | copy-start | bytes 1572868
  472.5 16.8 %copy-start.2 = (f32[896,1024]{1,0:T(8,128)S(1)}, f32[896,1024]{1,0:T(8,128)}, u32[]{:S(2)}) copy-start(f32[896,1024]{1,0:T(8,128)} %broadcast_multiply_fusion) | copy-start | bytes 11010052
  472.5 16.8 %copy-start.5 = (bf16[2048,1024]{1,0:T(8,128)(2,1)S(1)}, bf16[2048,1024]{1,0:T(8,128)(2,1)}, u32[]{:S(2)}) copy-start(bf16[2048,1024]{1,0:T(8,128)(2,1)} %param.4) | copy-start | bytes 12582916
Sparse Core Ops, SparseCore 0:
  8.9 50.5 all-gather.8
  70.3 101.8 all-reduce.2
  286.6 26.3 all-gather.10
  316.5 28.5 all-gather.12
  348.5 28.5 all-gather.14
  378.6 47.2 all-gather.6
  427.4 45.0 all-gather.16
